TPU v7x, 32 devices: a whole 2x2x4 slice. The times are simulated.
32 devices in a mesh: slab: 8 (over y, x, core), coil: 4 (over z).
Axes of the slice: x: 2, y: 2, z: 4, core: 2. Of those that a mesh axis runs over, the one named last changes fastest.
Arguments:
- sensitivity: float32 [4, 2, 16, 256, 128], P('coil', None, 'slab'), may hold values from -4 to 4
- kspace: float32 [4, 2, 16, 256, 128], P('coil', None, 'slab')
- sampling: int32 [16, 256, 128], P('slab'), may hold values 0 or 1
- prior_image: float32 [2, 16, 256, 128], P(None, 'slab', 'coil')
- w_first: bfloat16 [32, 2, 3, 3, 3], replicated, may hold values from -0.875 to 0.875
- w_middle: bfloat16 [3, 32, 32, 3, 3, 3], replicated, may hold values from -0.21875 to 0.21875
- w_last: bfloat16 [2, 32, 3, 3, 3], replicated, may hold values from -0.21875 to 0.21875
Outputs:
- solution: float32 [2, 16, 256, 128], P(None, 'slab', 'coil')
- refined: float32 [2, 16, 256, 128], P(None, 'slab', 'coil')
Inputs may be any that keep to these rules, and one draw needn't show every extreme that they name: sampling marks the measured ky-kz positions of each readout plane.
All inputs are finite; a program needn't handle non-finite values. No bound on the sum of `sampling` on one device may be relied on, other than what follows from the above.
Results may differ from a plain program's by a relative error of at most 0.0015.
Values may be sent and summed in bfloat16 or wider, within the bound.
A program may use at most 128 MiB of HBM per device.

v0:
```python
import math
import jax
import jax.numpy as jnp
from jax import lax
from jax.sharding import PartitionSpec as P

ITERS = 2
LAMBDA = 0.5
HIGHEST = lax.Precision.HIGHEST


def extended(cells, sides, width):
    for axis, dim in sides:
        count = lax.axis_size(axis)
        ends = count - 1
        head = lax.slice_in_dim(cells, 0, width, axis=dim)
        tail = lax.slice_in_dim(cells, cells.shape[dim] - width, cells.shape[dim], axis=dim)
        cells = jnp.concatenate(
            [
                lax.ppermute(tail, axis, [(i, (i + 1) % count) for i in range(ends)]),
                cells,
                lax.ppermute(head, axis, [((i + 1) % count, i) for i in range(ends)]),
            ],
            axis=dim,
        )
    return cells


def dft_tables(length, sign):
    positions = jnp.arange(length, dtype=jnp.int32)
    phases = positions[:, None] * positions[None, :] % length
    angles = 2.0 * math.pi / length * phases.astype(jnp.float32)
    scaling = 1.0 / math.sqrt(length)
    return (jnp.cos(angles) * scaling, sign * scaling * jnp.sin(angles))


def transform(field, tables):
    cosine_y, sine_y, cosine_z, sine_z = tables
    plain = jnp.einsum("ky,acpyz->acpkz", cosine_y, field, precision=HIGHEST)
    turned = jnp.einsum("ky,acpyz->acpkz", sine_y, field, precision=HIGHEST)
    field = jnp.stack([plain[0] - turned[1], plain[1] + turned[0]])
    plain = jnp.einsum("acpyz,zk->acpyk", field, cosine_z, precision=HIGHEST)
    turned = jnp.einsum("acpyz,zk->acpyk", field, sine_z, precision=HIGHEST)
    return jnp.stack([plain[0] - turned[1], plain[1] + turned[0]])


def combine_coils(field, coil_maps):
    real_part = jnp.sum(coil_maps[0] * field[0] + coil_maps[1] * field[1], axis=0)
    imag_part = jnp.sum(coil_maps[0] * field[1] - coil_maps[1] * field[0], axis=0)
    return jnp.stack([real_part, imag_part])


def coil_terms(image, coil_maps, mask_f, forward, backward):
    image_re = image[0][None]
    image_im = image[1][None]
    coil_field = jnp.stack(
        [
            coil_maps[0] * image_re - coil_maps[1] * image_im,
            coil_maps[0] * image_im + coil_maps[1] * image_re,
        ]
    )
    spectrum = transform(coil_field, forward) * mask_f
    energy = jnp.sum(spectrum * spectrum)
    return (combine_coils(transform(spectrum, backward), coil_maps), energy)


def coil_total(local_image):
    return lax.psum(local_image, "coil")


def image_total(value):
    return lax.psum(value, "slab")


def curvature(direction, energy):
    weight_share = LAMBDA / lax.axis_size("coil")
    local_sum = energy + weight_share * jnp.sum(direction * direction)
    return lax.psum(local_sum, ("slab", "coil"))


def shift_right(values):
    zero_column = jnp.zeros(values.shape[:-1] + (1,), values.dtype)
    return jnp.concatenate([zero_column, values[..., :-1]], axis=-1)


def shift_left(values):
    zero_column = jnp.zeros(values.shape[:-1] + (1,), values.dtype)
    return jnp.concatenate([values[..., 1:], zero_column], axis=-1)


def conv_layer(activation, weight):
    padded = extended(activation, (("slab", 1), ("coil", 2)), 1)
    plane_count = activation.shape[1]
    row_count = activation.shape[2]
    out_channels = weight.shape[0]
    totals = [
        jnp.zeros((out_channels,) + activation.shape[1:], jnp.float32) for offset_z in range(3)
    ]
    for shift_x in range(3):
        for shift_y in range(3):
            window = padded[:, shift_x : shift_x + plane_count, shift_y : shift_y + row_count, :]
            tap_weights = weight[:, :, shift_x, shift_y, :]
            stacked = jnp.einsum(
                "oit,ipyz->topyz", tap_weights, window, preferred_element_type=jnp.float32
            )
            for offset_z in range(3):
                totals[offset_z] = totals[offset_z] + stacked[offset_z]
    return totals[1] + shift_right(totals[0]) + shift_left(totals[2])


def body(sensitivity, kspace, sampling, prior_image, w_first, w_middle, w_last):
    coil_maps = jnp.moveaxis(sensitivity, 1, 0)
    measured = jnp.moveaxis(kspace, 1, 0)
    mask_f = sampling.astype(jnp.float32)
    len_y = coil_maps.shape[3]
    len_z = coil_maps.shape[4]
    forward = dft_tables(len_y, -1.0) + dft_tables(len_z, -1.0)
    backward = dft_tables(len_y, 1.0) + dft_tables(len_z, 1.0)
    block_rows = prior_image.shape[2]
    prior_view = lax.all_gather(prior_image, "coil", axis=2, tiled=True)
    adjoint_local = combine_coils(transform(measured * mask_f, backward), coil_maps)
    rhs = coil_total(adjoint_local) + LAMBDA * prior_view
    solution = jnp.zeros_like(rhs)
    residual = rhs
    direction = rhs
    norm_now = image_total(jnp.sum(residual * residual))
    for step_index in range(ITERS):
        local_q, energy = coil_terms(direction, coil_maps, mask_f, forward, backward)
        image_q = coil_total(local_q) + LAMBDA * direction
        step_size = norm_now / curvature(direction, energy)
        solution = solution + step_size * direction
        if step_index + 1 < ITERS:
            residual = residual - step_size * image_q
            norm_next = image_total(jnp.sum(residual * residual))
            direction = residual + norm_next / norm_now * direction
            norm_now = norm_next
    brick = lax.dynamic_slice_in_dim(solution, lax.axis_index("coil") * block_rows, block_rows, 2)
    features = brick.astype(jnp.bfloat16)
    hidden = jax.nn.relu(conv_layer(features, w_first)).astype(jnp.bfloat16)
    for layer_index in range(w_middle.shape[0]):
        hidden = jax.nn.relu(conv_layer(hidden, w_middle[layer_index])).astype(jnp.bfloat16)
    correction = conv_layer(hidden, w_last)
    return (brick, brick + correction)


def solution(mesh):
    placed = (
        P("coil", None, "slab", None, None),
        P("coil", None, "slab", None, None),
        P("slab", None, None),
        P(None, "slab", "coil", None),
        P(),
        P(),
        P(),
    )
    return jax.shard_map(
        body,
        mesh=mesh,
        in_specs=placed,
        out_specs=(P(None, "slab", "coil", None), P(None, "slab", "coil", None)),
        check_vma=False,
    )
```

profile of v0, /device:TPU:6, one launch (start us, length us, event | category | flops | bytes accessed | tf_op | source)
XLA Modules:
  0.0 498.4 jit_solution(12519650154397475423)
XLA Ops:
  17.3 22.0 %all_gather.3 = f32[2,2,256,128]{3,2,1,0:T(8,128)S(1)} all-gather(f32[2,2,64,128]{3,2,1,0:T(8,128)S(1)} %copy-done.6), channel_id=1, replica_groups=mesh['slab'=8,'coil'=4] {'coil'}, dimensions={2}, use_global_device_ids=true | all-gather | bytes 655360 | tf_op jit(solution)/shard_map/all_gather | solution.py:120
  39.3 21.7 %all-reduce.13.cloned.1.call-done = f32[2,2,256,128]{3,2,1,0:T(8,128)} async-done(((f32[2,2,256,128]{3,2,1,0:T(8,128)}), f32[2,2,256,128]{3,2,1,0:T(8,128)}) %all-reduce.13.cloned.1.call-update) | async-done | bytes 524304 | tf_op jit(solution)/shard_map/psum | solution.py:68
  78.4 40.5 %psum.44 = f32[]{:T(128)} all-reduce(f32[]{:T(128)S(6)} %add.651), channel_id=1, replica_groups=mesh['slab'=8,'coil'=4] {'slab','coil'}, use_global_device_ids=true, to_apply=%region_4.5 | all-reduce | flops 1 | bytes 8 | tf_op jit(solution)/shard_map/psum | solution.py:78
  118.9 10.9 %psum.43 = f32[]{:T(128)} all-reduce(f32[]{:T(128)} %get-tuple-element.6), channel_id=1, replica_groups=mesh['slab'=8,'coil'=4] {'slab'}, use_global_device_ids=true, to_apply=%region_2.3 | all-reduce | flops 1 | bytes 8 | tf_op jit(solution)/shard_map/psum | solution.py:72
  133.0 13.2 %psum.46 = f32[]{:T(128)} all-reduce(f32[]{:T(128)} %multiply_reduce_fusion.1), channel_id=1, replica_groups=mesh['slab'=8,'coil'=4] {'slab'}, use_global_device_ids=true, to_apply=%region_7.8 | all-reduce | flops 1 | bytes 8 | tf_op jit(solution)/shard_map/psum | solution.py:72
  157.5 40.9 %psum.47 = f32[]{:T(128)} all-reduce(f32[]{:T(128)S(6)} %add.660), channel_id=1, replica_groups=mesh['slab'=8,'coil'=4] {'slab','coil'}, use_global_device_ids=true, to_apply=%region_10.11 | all-reduce | flops 1 | bytes 8 | tf_op jit(solution)/shard_map/psum | solution.py:78
  232.3 3.7 convolution_bitcast_fusion.35
  236.1 5.2 %fusion.22 = f32[32,2,64,128]{3,0,2,1:T(8,128)S(1)} fusion(f32[3,32,2,64,128]{4,1,3,2,0:T(8,128)S(1)} %convolution_bitcast_fusion.27, f32[3,32,2,64,128]{4,1,3,2,0:T(8,128)S(1)} %convolution_bitcast_fusion.28, f32[3,32,2,64,128]{4,1,3,2,0:T(8,128)} %convolution_bitcast_fusion.29, f32[3,32,2,64,128]{4,1,3,2,0:T(8,128)} %convolution_bitcast_fusion.30, ...), kind=kLoop, calls=%fused_computation.139 | loop fusion | flops 4194304 | bytes 20971520 | tf_op jit(solution)/shard_map/add | solution.py:107
  241.3 5.2 %fusion.30 = f32[32,2,64,128]{3,0,2,1:T(8,128)S(1)} fusion(f32[3,32,2,64,128]{4,1,3,2,0:T(8,128)S(1)} %convolution_bitcast_fusion.27, f32[3,32,2,64,128]{4,1,3,2,0:T(8,128)S(1)} %convolution_bitcast_fusion.28, f32[3,32,2,64,128]{4,1,3,2,0:T(8,128)} %convolution_bitcast_fusion.29, f32[3,32,2,64,128]{4,1,3,2,0:T(8,128)} %convolution_bitcast_fusion.30, ...), kind=kLoop, calls=%fused_computation.155 | loop fusion | flops 4194304 | bytes 20971520 | tf_op jit(solution)/shard_map/add | solution.py:107
  247.1 5.4 %fusion.35 = bf16[32,2,64,128]{3,0,2,1:T(8,128)(2,1)S(1)} fusion(f32[3,32,2,64,128]{4,1,3,2,0:T(8,128)S(1)} %convolution_bitcast_fusion.27, f32[3,32,2,64,128]{4,1,3,2,0:T(8,128)S(1)} %convolution_bitcast_fusion.28, f32[3,32,2,64,128]{4,1,3,2,0:T(8,128)} %convolution_bitcast_fusion.29, f32[3,32,2,64,128]{4,1,3,2,0:T(8,128)} %convolution_bitcast_fusion.30, ...), kind=kLoop, calls=%fused_computation.169 | loop fusion | flops 6291456 | bytes 24084480 | tf_op jit(solution)/shard_map/convert_element_type | solution.py:139
  261.4 7.6 %collective-permute-done.4 = bf16[32,1,64,128]{3,0,2,1:T(8,128)(2,1)S(1)} collective-permute-done((bf16[32,1,64,128]{3,0,2,1:T(8,128)(2,1)S(1)}, bf16[32,1,64,128]{3,0,2,1:T(8,128)(2,1)S(1)}, u32[]{:S(2)}, u32[]{:S(2)}) %collective-permute-start.4) | collective-permute-done | bytes 524320 | tf_op jit(solution)/shard_map/ppermute | solution.py:20
  300.2 13.8 %fusion.15 = (f32[32,2,64,128]{3,0,2,1:T(8,128)}, f32[32,2,64,128]{3,0,2,1:T(8,128)}) fusion(f32[3,32,2,64,128]{4,1,3,2,0:T(8,128)} %convolution_bitcast_fusion.18, f32[3,32,2,64,128]{4,1,3,2,0:T(8,128)S(1)} %convolution_bitcast_fusion.19, f32[3,32,2,64,128]{4,1,3,2,0:T(8,128)} %convolution_bitcast_fusion.20, ...), kind=kLoop, calls=%fused_computation.116 | loop fusion | flops 8388608 | bytes 41943040 | tf_op jit(solution)/shard_map/add | solution.py:107
  316.4 6.6 %fusion.20 = bf16[32,2,64,128]{3,0,2,1:T(8,128)(2,1)S(1)} fusion(f32[3,32,2,64,128]{4,1,3,2,0:T(8,128)} %convolution_bitcast_fusion.18, f32[3,32,2,64,128]{4,1,3,2,0:T(8,128)S(1)} %convolution_bitcast_fusion.19, f32[3,32,2,64,128]{4,1,3,2,0:T(8,128)} %convolution_bitcast_fusion.20, f32[3,32,2,64,128]{4,1,3,2,0:T(8,128)} %convolution_bitcast_fusion.21, ...), kind=kLoop, calls=%fused_computation.129 | loop fusion | flops 6291456 | bytes 24084480 | tf_op jit(solution)/shard_map/convert_element_type | solution.py:141
  331.7 6.4 %collective-permute-done.8 = bf16[32,1,64,128]{3,0,2,1:T(8,128)(2,1)S(1)} collective-permute-done((bf16[32,1,64,128]{3,0,2,1:T(8,128)(2,1)S(1)}, bf16[32,1,64,128]{3,0,2,1:T(8,128)(2,1)S(1)}, u32[]{:S(2)}, u32[]{:S(2)}) %collective-permute-start.8) | collective-permute-done | bytes 524320 | tf_op jit(solution)/shard_map/ppermute | solution.py:20
  338.1 4.5 collective-permute-start.10
  370.9 13.8 %fusion.8 = (f32[32,2,64,128]{3,0,2,1:T(8,128)}, f32[32,2,64,128]{3,0,2,1:T(8,128)}) fusion(f32[3,32,2,64,128]{4,1,3,2,0:T(8,128)} %convolution_bitcast_fusion.9, f32[3,32,2,64,128]{4,1,3,2,0:T(8,128)S(1)} %convolution_bitcast_fusion.10, f32[3,32,2,64,128]{4,1,3,2,0:T(8,128)} %convolution_bitcast_fusion.11, ...), kind=kLoop, calls=%fused_computation.85 | loop fusion | flops 8388608 | bytes 41943040 | tf_op jit(solution)/shard_map/add | solution.py:107
  387.1 6.6 %fusion.13 = bf16[32,2,64,128]{3,0,2,1:T(8,128)(2,1)S(1)} fusion(f32[3,32,2,64,128]{4,1,3,2,0:T(8,128)} %convolution_bitcast_fusion.9, f32[3,32,2,64,128]{4,1,3,2,0:T(8,128)S(1)} %convolution_bitcast_fusion.10, f32[3,32,2,64,128]{4,1,3,2,0:T(8,128)} %convolution_bitcast_fusion.11, f32[3,32,2,64,128]{4,1,3,2,0:T(8,128)} %convolution_bitcast_fusion.12, ...), kind=kLoop, calls=%fused_computation.98 | loop fusion | flops 6291456 | bytes 24084480 | tf_op jit(solution)/shard_map/convert_element_type | solution.py:141
  402.3 5.1 %collective-permute-done.12 = bf16[32,1,64,128]{3,0,2,1:T(8,128)(2,1)S(1)} collective-permute-done((bf16[32,1,64,128]{3,0,2,1:T(8,128)(2,1)S(1)}, bf16[32,1,64,128]{3,0,2,1:T(8,128)(2,1)S(1)}, u32[]{:S(2)}, u32[]{:S(2)}) %collective-permute-start.12) | collective-permute-done | bytes 524320 | tf_op jit(solution)/shard_map/ppermute | solution.py:20
  407.5 4.3 collective-permute-start.14
  439.9 13.8 %fusion.1 = (f32[32,2,64,128]{3,0,2,1:T(8,128)}, f32[32,2,64,128]{3,0,2,1:T(8,128)}) fusion(f32[3,32,2,64,128]{4,1,3,2,0:T(8,128)} %convolution_bitcast_fusion, f32[3,32,2,64,128]{4,1,3,2,0:T(8,128)S(1)} %convolution_bitcast_fusion.1, f32[3,32,2,64,128]{4,1,3,2,0:T(8,128)} %convolution_bitcast_fusion.2, f32[3,32,2,64,128]{4,1,3,2,0:T(8,128)} %convolution_bitcast_fusion.3, ...), kind=kLoop, calls=%fused_computation.54 | loop fusion | flops 8388608 | bytes 41943040 | tf_op jit(solution)/shard_map/add | solution.py:107
  456.1 6.6 %fusion.6 = bf16[32,2,64,128]{3,0,2,1:T(8,128)(2,1)S(1)} fusion(f32[3,32,2,64,128]{4,1,3,2,0:T(8,128)} %convolution_bitcast_fusion, f32[3,32,2,64,128]{4,1,3,2,0:T(8,128)S(1)} %convolution_bitcast_fusion.1, f32[3,32,2,64,128]{4,1,3,2,0:T(8,128)} %convolution_bitcast_fusion.2, f32[3,32,2,64,128]{4,1,3,2,0:T(8,128)} %convolution_bitcast_fusion.3, ...), kind=kLoop, calls=%fused_computation.67 | loop fusion | flops 6291456 | bytes 24084480 | tf_op jit(solution)/shard_map/convert_element_type | solution.py:141
  467.6 3.8 collective-permute-done.17
  471.4 4.7 collective-permute-done.16
  476.2 4.6 collective-permute-start.18
  (169 shorter events, 205.1 us)
Async XLA Ops:
  7.2 53.9 %all-reduce.13.cloned.1.call-start = ((), (), s32[]{:S(2)}) async-start(), calls=%async_computation | async-start | bytes 1048576 | tf_op jit(solution)/shard_map/psum | solution.py:68
  17.3 113.9 %all-reduce.15.cloned.1.call-start = ((), (), s32[]{:S(2)}) async-start(), calls=%async_computation.1 | async-start | bytes 1048576 | tf_op jit(solution)/shard_map/psum | solution.py:68
  154.3 50.5 %copy-start.7 = (bf16[32,2,3,3,3]{0,1,4,3,2:T(2,128)(2,1)S(1)}, bf16[32,2,3,3,3]{0,1,4,3,2:T(2,128)(2,1)}, u32[]{:S(2)}) copy-start(bf16[32,2,3,3,3]{0,1,4,3,2:T(2,128)(2,1)} %param.11) | copy-start | bytes 10372
  200.5 5.4 %collective-permute-start.1 = (bf16[2,1,64,128]{3,2,1,0:T(8,128)(2,1)S(1)}, bf16[2,1,64,128]{3,2,1,0:T(8,128)(2,1)S(1)}, u32[]{:S(2)}, u32[]{:S(2)}) collective-permute-start(bf16[2,1,64,128]{3,2,1,0:T(8,128)(2,1)S(1)} %get-tuple-element.76), channel_id=1, source_target_pairs={{4,0},{8,4},{12,8},{16,12},{20,16},{24,20},{28,24},{5,1},{9,5},{13... | collective-permute-start | bytes 98312 | tf_op jit(solution)/shard_map/ppermute | solution.py:22
  202.4 5.2 %collective-permute-start = (bf16[2,1,64,128]{3,2,1,0:T(8,128)(2,1)S(1)}, bf16[2,1,64,128]{3,2,1,0:T(8,128)(2,1)S(1)}, u32[]{:S(2)}, u32[]{:S(2)}) collective-permute-start(bf16[2,1,64,128]{3,2,1,0:T(8,128)(2,1)S(1)} %get-tuple-element.75), channel_id=1, source_target_pairs={{0,4},{4,8},{8,12},{12,16},{16,20},{20,24},{24,28},{1,5},{5,9},{9,... | collective-permute-start | bytes 98312 | tf_op jit(solution)/shard_map/ppermute | solution.py:20
  207.7 7.0 %collective-permute-start.2 = (bf16[2,4,1,128]{3,2,1,0:T(2,128)(2,1)S(1)}, bf16[2,4,1,128]{3,2,1,0:T(2,128)(2,1)S(1)}, u32[]{:S(2)}, u32[]{:S(2)}) collective-permute-start(bf16[2,4,1,128]{3,2,1,0:T(2,128)(2,1)S(1)} %get-tuple-element.71), channel_id=1, source_target_pairs={{0,1},{1,2},{2,3},{4,5},{5,6},{6,7},{8,9},{9,10},{10,11},{12,13},{... | collective-permute-start | bytes 6152 | tf_op jit(solution)/shard_map/ppermute | solution.py:20
  211.1 5.5 %collective-permute-start.3 = (bf16[2,4,1,128]{3,2,1,0:T(2,128)(2,1)S(1)}, bf16[2,4,1,128]{3,2,1,0:T(2,128)(2,1)S(1)}, u32[]{:S(2)}, u32[]{:S(2)}) collective-permute-start(bf16[2,4,1,128]{3,2,1,0:T(2,128)(2,1)S(1)} %get-tuple-element.72), channel_id=1, source_target_pairs={{1,0},{2,1},{3,2},{5,4},{6,5},{7,6},{9,8},{10,9},{11,10},{13,12},{... | collective-permute-start | bytes 6152 | tf_op jit(solution)/shard_map/ppermute | solution.py:22
  252.5 4.6 copy-start.4
  252.6 8.7 %collective-permute-start.5 = (bf16[32,1,64,128]{3,0,2,1:T(8,128)(2,1)S(1)}, bf16[32,1,64,128]{3,0,2,1:T(8,128)(2,1)S(1)}, u32[]{:S(2)}, u32[]{:S(2)}) collective-permute-start(bf16[32,1,64,128]{3,0,2,1:T(8,128)(2,1)S(1)} %get-tuple-element.43), channel_id=1, source_target_pairs={{4,0},{8,4},{12,8},{16,12},{20,16},{24,20},{28,24},{5,1},{9,5},{13... | collective-permute-start | bytes 1572872 | tf_op jit(solution)/shard_map/ppermute | solution.py:22
  254.7 14.3 %collective-permute-start.4 = (bf16[32,1,64,128]{3,0,2,1:T(8,128)(2,1)S(1)}, bf16[32,1,64,128]{3,0,2,1:T(8,128)(2,1)S(1)}, u32[]{:S(2)}, u32[]{:S(2)}) collective-permute-start(bf16[32,1,64,128]{3,0,2,1:T(8,128)(2,1)S(1)} %get-tuple-element.42), channel_id=1, source_target_pairs={{0,4},{4,8},{8,12},{12,16},{16,20},{20,24},{24,28},{1,5},{5,9},{9,... | collective-permute-start | bytes 1572872 | tf_op jit(solution)/shard_map/ppermute | solution.py:20
  269.0 8.9 %collective-permute-start.6 = (bf16[32,4,1,128]{3,0,2,1:T(8,128)(2,1)S(1)}, bf16[32,4,1,128]{3,0,2,1:T(8,128)(2,1)S(1)}, u32[]{:S(2)}, u32[]{:S(2)}) collective-permute-start(bf16[32,4,1,128]{3,0,2,1:T(8,128)(2,1)S(1)} %get-tuple-element.30), channel_id=1, source_target_pairs={{0,1},{1,2},{2,3},{4,5},{5,6},{6,7},{8,9},{9,10},{10,11},{12,13},{... | collective-permute-start | bytes 98312 | tf_op jit(solution)/shard_map/ppermute | solution.py:20
  272.0 5.9 %collective-permute-start.7 = (bf16[32,4,1,128]{3,0,2,1:T(8,128)(2,1)S(1)}, bf16[32,4,1,128]{3,0,2,1:T(8,128)(2,1)S(1)}, u32[]{:S(2)}, u32[]{:S(2)}) collective-permute-start(bf16[32,4,1,128]{3,0,2,1:T(8,128)(2,1)S(1)} %get-tuple-element.31), channel_id=1, source_target_pairs={{1,0},{2,1},{3,2},{5,4},{6,5},{7,6},{9,8},{10,9},{11,10},{13,12},{... | collective-permute-start | bytes 98312 | tf_op jit(solution)/shard_map/ppermute | solution.py:22
  323.1 8.6 %collective-permute-start.9 = (bf16[32,1,64,128]{3,0,2,1:T(8,128)(2,1)S(1)}, bf16[32,1,64,128]{3,0,2,1:T(8,128)(2,1)S(1)}, u32[]{:S(2)}, u32[]{:S(2)}) collective-permute-start(bf16[32,1,64,128]{3,0,2,1:T(8,128)(2,1)S(1)} %get-tuple-element.41), channel_id=1, source_target_pairs={{4,0},{8,4},{12,8},{16,12},{20,16},{24,20},{28,24},{5,1},{9,5},{13... | collective-permute-start | bytes 1572872 | tf_op jit(solution)/shard_map/ppermute | solution.py:22
  325.0 13.1 %collective-permute-start.8 = (bf16[32,1,64,128]{3,0,2,1:T(8,128)(2,1)S(1)}, bf16[32,1,64,128]{3,0,2,1:T(8,128)(2,1)S(1)}, u32[]{:S(2)}, u32[]{:S(2)}) collective-permute-start(bf16[32,1,64,128]{3,0,2,1:T(8,128)(2,1)S(1)} %get-tuple-element.40), channel_id=1, source_target_pairs={{0,4},{4,8},{8,12},{12,16},{16,20},{20,24},{24,28},{1,5},{5,9},{9,... | collective-permute-start | bytes 1572872 | tf_op jit(solution)/shard_map/ppermute | solution.py:20
  338.1 10.5 %collective-permute-start.10 = (bf16[32,4,1,128]{3,0,2,1:T(8,128)(2,1)S(1)}, bf16[32,4,1,128]{3,0,2,1:T(8,128)(2,1)S(1)}, u32[]{:S(2)}, u32[]{:S(2)}) collective-permute-start(bf16[32,4,1,128]{3,0,2,1:T(8,128)(2,1)S(1)} %get-tuple-element.26), channel_id=1, source_target_pairs={{0,1},{1,2},{2,3},{4,5},{5,6},{6,7},{8,9},{9,10},{10,11},{12,13},{... | collective-permute-start | bytes 98312 | tf_op jit(solution)/shard_map/ppermute | solution.py:20
  342.7 5.9 %collective-permute-start.11 = (bf16[32,4,1,128]{3,0,2,1:T(8,128)(2,1)S(1)}, bf16[32,4,1,128]{3,0,2,1:T(8,128)(2,1)S(1)}, u32[]{:S(2)}, u32[]{:S(2)}) collective-permute-start(bf16[32,4,1,128]{3,0,2,1:T(8,128)(2,1)S(1)} %get-tuple-element.27), channel_id=1, source_target_pairs={{1,0},{2,1},{3,2},{5,4},{6,5},{7,6},{9,8},{10,9},{11,10},{13,12},{... | collective-permute-start | bytes 98312 | tf_op jit(solution)/shard_map/ppermute | solution.py:22
  393.7 8.6 %collective-permute-start.13 = (bf16[32,1,64,128]{3,0,2,1:T(8,128)(2,1)S(1)}, bf16[32,1,64,128]{3,0,2,1:T(8,128)(2,1)S(1)}, u32[]{:S(2)}, u32[]{:S(2)}) collective-permute-start(bf16[32,1,64,128]{3,0,2,1:T(8,128)(2,1)S(1)} %get-tuple-element.39), channel_id=1, source_target_pairs={{4,0},{8,4},{12,8},{16,12},{20,16},{24,20},{28,24},{5,1},{9,5},{13... | collective-permute-start | bytes 1572872 | tf_op jit(solution)/shard_map/ppermute | solution.py:22
  395.7 11.8 %collective-permute-start.12 = (bf16[32,1,64,128]{3,0,2,1:T(8,128)(2,1)S(1)}, bf16[32,1,64,128]{3,0,2,1:T(8,128)(2,1)S(1)}, u32[]{:S(2)}, u32[]{:S(2)}) collective-permute-start(bf16[32,1,64,128]{3,0,2,1:T(8,128)(2,1)S(1)} %get-tuple-element.38), channel_id=1, source_target_pairs={{0,4},{4,8},{8,12},{12,16},{16,20},{20,24},{24,28},{1,5},{5,9},{9,... | collective-permute-start | bytes 1572872 | tf_op jit(solution)/shard_map/ppermute | solution.py:20
  407.5 10.2 %collective-permute-start.14 = (bf16[32,4,1,128]{3,0,2,1:T(8,128)(2,1)S(1)}, bf16[32,4,1,128]{3,0,2,1:T(8,128)(2,1)S(1)}, u32[]{:S(2)}, u32[]{:S(2)}) collective-permute-start(bf16[32,4,1,128]{3,0,2,1:T(8,128)(2,1)S(1)} %get-tuple-element.22), channel_id=1, source_target_pairs={{0,1},{1,2},{2,3},{4,5},{5,6},{6,7},{8,9},{9,10},{10,11},{12,13},{... | collective-permute-start | bytes 98312 | tf_op jit(solution)/shard_map/ppermute | solution.py:20
  411.7 5.9 %collective-permute-start.15 = (bf16[32,4,1,128]{3,0,2,1:T(8,128)(2,1)S(1)}, bf16[32,4,1,128]{3,0,2,1:T(8,128)(2,1)S(1)}, u32[]{:S(2)}, u32[]{:S(2)}) collective-permute-start(bf16[32,4,1,128]{3,0,2,1:T(8,128)(2,1)S(1)} %get-tuple-element.23), channel_id=1, source_target_pairs={{1,0},{2,1},{3,2},{5,4},{6,5},{7,6},{9,8},{10,9},{11,10},{13,12},{... | collective-permute-start | bytes 98312 | tf_op jit(solution)/shard_map/ppermute | solution.py:22
  462.8 8.6 %collective-permute-start.17 = (bf16[32,1,64,128]{3,0,2,1:T(8,128)(2,1)S(1)}, bf16[32,1,64,128]{3,0,2,1:T(8,128)(2,1)S(1)}, u32[]{:S(2)}, u32[]{:S(2)}) collective-permute-start(bf16[32,1,64,128]{3,0,2,1:T(8,128)(2,1)S(1)} %get-tuple-element.37), channel_id=1, source_target_pairs={{4,0},{8,4},{12,8},{16,12},{20,16},{24,20},{28,24},{5,1},{9,5},{13... | collective-permute-start | bytes 1572872 | tf_op jit(solution)/shard_map/ppermute | solution.py:22
  464.8 11.4 %collective-permute-start.16 = (bf16[32,1,64,128]{3,0,2,1:T(8,128)(2,1)S(1)}, bf16[32,1,64,128]{3,0,2,1:T(8,128)(2,1)S(1)}, u32[]{:S(2)}, u32[]{:S(2)}) collective-permute-start(bf16[32,1,64,128]{3,0,2,1:T(8,128)(2,1)S(1)} %get-tuple-element.36), channel_id=1, source_target_pairs={{0,4},{4,8},{8,12},{12,16},{16,20},{20,24},{24,28},{1,5},{5,9},{9,... | collective-permute-start | bytes 1572872 | tf_op jit(solution)/shard_map/ppermute | solution.py:20
  476.2 6.9 %collective-permute-start.18 = (bf16[32,4,1,128]{3,0,2,1:T(8,128)(2,1)S(1)}, bf16[32,4,1,128]{3,0,2,1:T(8,128)(2,1)S(1)}, u32[]{:S(2)}, u32[]{:S(2)}) collective-permute-start(bf16[32,4,1,128]{3,0,2,1:T(8,128)(2,1)S(1)} %get-tuple-element.18), channel_id=1, source_target_pairs={{0,1},{1,2},{2,3},{4,5},{5,6},{6,7},{8,9},{9,10},{10,11},{12,13},{... | collective-permute-start | bytes 98312 | tf_op jit(solution)/shard_map/ppermute | solution.py:20
  480.7 5.8 %collective-permute-start.19 = (bf16[32,4,1,128]{3,0,2,1:T(8,128)(2,1)S(1)}, bf16[32,4,1,128]{3,0,2,1:T(8,128)(2,1)S(1)}, u32[]{:S(2)}, u32[]{:S(2)}) collective-permute-start(bf16[32,4,1,128]{3,0,2,1:T(8,128)(2,1)S(1)} %get-tuple-element.19), channel_id=1, source_target_pairs={{1,0},{2,1},{3,2},{5,4},{6,5},{7,6},{9,8},{10,9},{11,10},{13,12},{... | collective-permute-start | bytes 98312 | tf_op jit(solution)/shard_map/ppermute | solution.py:22
  (7 other events, 15.8 us)
Sparse Core Ops, SparseCore 0:
  17.4 43.5 all-reduce.12
  76.5 38.5 all-reduce.14
where the time goes:
time: 505 us; the launch traced here: 498 us
  matrix products  132 us (26%)
  blocking collectives  128 us (25%)
  other arithmetic  91.8 us (18%)
  waiting for transfers between devices  66.1 us (13%)
  starting transfers between devices  49.1 us (10%)
  between operations  22 us (4%)
  local copies, waits for them, and re-layouts  9.42 us (2%)
    dot_general x45, matrix products, conv_layer(): jnp.einsum('oit,ipyz->topyz', tap_weights, window, preferred_element_type...  106 us
    psum x2, blocking collectives, curvature(): return lax.psum(local_sum, ('slab', 'coil'))  81.4 us
    add x6, other arithmetic, conv_layer(): totals[offset_z] = totals[offset_z] + stacked[offset_z]  52.1 us
    ppermute x10, starting transfers between devices, extended(): lax.ppermute(tail, axis, [(i, (i + 1) % count) for i in range(ends)])  32.4 us
    ppermute x10, waiting for transfers between devices, extended(): lax.ppermute(tail, axis, [(i, (i + 1) % count) for i in range(ends)])  25.7 us
    psum x2, blocking collectives, image_total(): return lax.psum(value, 'slab')  24.2 us
    all_gather x1, blocking collectives, body(): prior_view = lax.all_gather(prior_image, 'coil', axis=2, tiled=True)  22 us
    psum x2, waiting for transfers between devices, coil_total(): return lax.psum(local_image, 'coil')  21.7 us
  transfers between devices with their start and end apart: 22, of which 12 were waited for; matrix products, arithmetic and copies ran while one was open for 4% of the time, Pallas kernels for 0%

commit v1 on v0

--- a/solution.py
+++ b/solution.py
@@ -7,6 +7,11 @@
 ITERS = 2
 LAMBDA = 0.5
 HIGHEST = lax.Precision.HIGHEST
+
+
+def axis_by_axis(value_2, first, second):
+    inner = lax.psum(value_2, first)
+    return lax.psum(inner, second)
 
 
 def extended(cells, sides, width):
@@ -75,7 +80,7 @@
 def curvature(direction, energy):
     weight_share = LAMBDA / lax.axis_size("coil")
     local_sum = energy + weight_share * jnp.sum(direction * direction)
-    return lax.psum(local_sum, ("slab", "coil"))
+    return axis_by_axis(local_sum, "slab", "coil")
 
 
 def shift_right(values):

time: 505 us -> 468 us (0.927)
  blocking collectives: 128 us -> 78 us
  waiting for transfers between devices: 66.1 us -> 81.4 us
    psum x2 -> x3, blocking collectives: 81.4 us -> 34.7 us  [the longest x2 22.4 us: axis_by_axis(): return lax.psum(inner, second)]
    psum x2, waiting for transfers between devices: 21.7 us -> 35.2 us  [coil_total(): return lax.psum(local_image, 'coil')]
  transfers between devices with their start and end apart: 22 -> 22, of which waited for: 12 -> 13; matrix products, arithmetic and copies ran while one was open for 4% -> 5% of each run, Pallas kernels for 0% -> 0%
where the time goes in v1:
time: 468 us; the launch traced here: 462 us
  matrix products  132 us (28%)
  other arithmetic  91.9 us (20%)
  waiting for transfers between devices  81.4 us (17%)
  blocking collectives  78 us (17%)
  starting transfers between devices  47.2 us (10%)
  between operations  22 us (5%)
  local copies, waits for them, and re-layouts  9.42 us (2%)
    dot_general x45, matrix products, conv_layer(): jnp.einsum('oit,ipyz->topyz', tap_weights, window, preferred_element_type...  106 us
    add x6, other arithmetic, conv_layer(): totals[offset_z] = totals[offset_z] + stacked[offset_z]  52.1 us
    psum x2, waiting for transfers between devices, coil_total(): return lax.psum(local_image, 'coil')  35.2 us
    ppermute x10, starting transfers between devices, extended(): lax.ppermute(tail, axis, [(i, (i + 1) % count) for i in range(ends)])  30.5 us
    ppermute x10, waiting for transfers between devices, extended(): lax.ppermute(tail, axis, [(i, (i + 1) % count) for i in range(ends)])  27.5 us
    psum x2, blocking collectives, axis_by_axis(): return lax.psum(inner, second)  22.4 us
    all_gather x1, blocking collectives, body(): prior_view = lax.all_gather(prior_image, 'coil', axis=2, tiled=True)  22 us
    psum x2, blocking collectives, image_total(): return lax.psum(value, 'slab')  21.3 us
  transfers between devices with their start and end apart: 22, of which 13 were waited for; matrix products, arithmetic and copies ran while one was open for 5% of the time, Pallas kernels for 0%

profile of v1, /device:TPU:6, one launch (start us, length us, event | category | flops | bytes accessed | tf_op | source)
XLA Modules:
  0.0 462.1 jit_solution(16886123190111998481)
XLA Ops:
  17.4 22.0 %all_gather.3 = f32[2,2,256,128]{3,2,1,0:T(8,128)S(1)} all-gather(f32[2,2,64,128]{3,2,1,0:T(8,128)S(1)} %copy-done.6), channel_id=1, replica_groups=mesh['slab'=8,'coil'=4] {'coil'}, dimensions={2}, use_global_device_ids=true | all-gather | bytes 655360 | tf_op jit(solution)/shard_map/all_gather | solution.py:125
  39.4 21.7 %all-reduce.14.cloned.1.call-done = f32[2,2,256,128]{3,2,1,0:T(8,128)} async-done(((f32[2,2,256,128]{3,2,1,0:T(8,128)}), f32[2,2,256,128]{3,2,1,0:T(8,128)}) %all-reduce.14.cloned.1.call-update) | async-done | bytes 524304 | tf_op jit(solution)/shard_map/psum | solution.py:73
  78.4 10.6 %all-reduce.10 = (f32[]{:T(128)}, f32[]{:T(128)}) all-reduce(f32[]{:T(128)} %get-tuple-element.8, f32[]{:T(128)S(6)} %add.655), channel_id=1, replica_groups=mesh['slab'=8,'coil'=4] {'slab'}, use_global_device_ids=true, to_apply=%region_2.3 | all-reduce | flops 2 | bytes 16 | tf_op jit(solution)/shard_map/psum | solution.py:77
  89.0 11.2 %psum.59 = f32[]{:T(128)} all-reduce(f32[]{:T(128)} %get-tuple-element.3), channel_id=1, replica_groups=mesh['slab'=8,'coil'=4] {'coil'}, use_global_device_ids=true, to_apply=%region_5.6 | all-reduce | flops 1 | bytes 8 | tf_op jit(solution)/shard_map/psum | solution.py:14
  101.6 13.5 %all-reduce.16.cloned.1.call-done = f32[2,2,256,128]{3,2,1,0:T(8,128)} async-done(((f32[2,2,256,128]{3,2,1,0:T(8,128)}), f32[2,2,256,128]{3,2,1,0:T(8,128)}) %all-reduce.16.cloned.1.call-update) | async-done | bytes 524304 | tf_op jit(solution)/shard_map/psum | solution.py:73
  116.9 10.6 %psum.61 = f32[]{:T(128)} all-reduce(f32[]{:T(128)} %multiply_reduce_fusion.1), channel_id=1, replica_groups=mesh['slab'=8,'coil'=4] {'slab'}, use_global_device_ids=true, to_apply=%region_8.9 | all-reduce | flops 1 | bytes 8 | tf_op jit(solution)/shard_map/psum | solution.py:77
  138.8 12.3 %psum.62 = f32[]{:T(128)} all-reduce(f32[]{:T(128)S(6)} %add.664), channel_id=1, replica_groups=mesh['slab'=8,'coil'=4] {'slab'}, use_global_device_ids=true, to_apply=%region_11.12 | all-reduce | flops 1 | bytes 8 | tf_op jit(solution)/shard_map/psum | solution.py:13
  151.2 11.2 %psum.63 = f32[]{:T(128)} all-reduce(f32[]{:T(128)} %psum.62), channel_id=1, replica_groups=mesh['slab'=8,'coil'=4] {'coil'}, use_global_device_ids=true, to_apply=%region_12.13 | all-reduce | flops 1 | bytes 8 | tf_op jit(solution)/shard_map/psum | solution.py:14
  198.8 5.2 %fusion.22 = f32[32,2,64,128]{3,0,2,1:T(8,128)S(1)} fusion(f32[3,32,2,64,128]{4,1,3,2,0:T(8,128)S(1)} %convolution_bitcast_fusion.27, f32[3,32,2,64,128]{4,1,3,2,0:T(8,128)S(1)} %convolution_bitcast_fusion.28, f32[3,32,2,64,128]{4,1,3,2,0:T(8,128)} %convolution_bitcast_fusion.29, f32[3,32,2,64,128]{4,1,3,2,0:T(8,128)} %convolution_bitcast_fusion.30, ...), kind=kLoop, calls=%fused_computation.139 | loop fusion | flops 4194304 | bytes 20971520 | tf_op jit(solution)/shard_map/add | solution.py:112
  204.0 5.2 %fusion.30 = f32[32,2,64,128]{3,0,2,1:T(8,128)S(1)} fusion(f32[3,32,2,64,128]{4,1,3,2,0:T(8,128)S(1)} %convolution_bitcast_fusion.27, f32[3,32,2,64,128]{4,1,3,2,0:T(8,128)S(1)} %convolution_bitcast_fusion.28, f32[3,32,2,64,128]{4,1,3,2,0:T(8,128)} %convolution_bitcast_fusion.29, f32[3,32,2,64,128]{4,1,3,2,0:T(8,128)} %convolution_bitcast_fusion.30, ...), kind=kLoop, calls=%fused_computation.155 | loop fusion | flops 4194304 | bytes 20971520 | tf_op jit(solution)/shard_map/add | solution.py:112
  209.9 5.4 %fusion.35 = bf16[32,2,64,128]{3,0,2,1:T(8,128)(2,1)S(1)} fusion(f32[3,32,2,64,128]{4,1,3,2,0:T(8,128)S(1)} %convolution_bitcast_fusion.27, f32[3,32,2,64,128]{4,1,3,2,0:T(8,128)S(1)} %convolution_bitcast_fusion.28, f32[3,32,2,64,128]{4,1,3,2,0:T(8,128)} %convolution_bitcast_fusion.29, f32[3,32,2,64,128]{4,1,3,2,0:T(8,128)} %convolution_bitcast_fusion.30, ...), kind=kLoop, calls=%fused_computation.169 | loop fusion | flops 6291456 | bytes 24084480 | tf_op jit(solution)/shard_map/convert_element_type | solution.py:144
  224.1 8.6 %collective-permute-done.4 = bf16[32,1,64,128]{3,0,2,1:T(8,128)(2,1)S(1)} collective-permute-done((bf16[32,1,64,128]{3,0,2,1:T(8,128)(2,1)S(1)}, bf16[32,1,64,128]{3,0,2,1:T(8,128)(2,1)S(1)}, u32[]{:S(2)}, u32[]{:S(2)}) %collective-permute-start.4) | collective-permute-done | bytes 524320 | tf_op jit(solution)/shard_map/ppermute | solution.py:25
  263.9 13.9 %fusion.15 = (f32[32,2,64,128]{3,0,2,1:T(8,128)}, f32[32,2,64,128]{3,0,2,1:T(8,128)}) fusion(f32[3,32,2,64,128]{4,1,3,2,0:T(8,128)} %convolution_bitcast_fusion.18, f32[3,32,2,64,128]{4,1,3,2,0:T(8,128)S(1)} %convolution_bitcast_fusion.19, f32[3,32,2,64,128]{4,1,3,2,0:T(8,128)} %convolution_bitcast_fusion.20, ...), kind=kLoop, calls=%fused_computation.116 | loop fusion | flops 8388608 | bytes 41943040 | tf_op jit(solution)/shard_map/add | solution.py:112
  280.1 6.6 %fusion.20 = bf16[32,2,64,128]{3,0,2,1:T(8,128)(2,1)S(1)} fusion(f32[3,32,2,64,128]{4,1,3,2,0:T(8,128)} %convolution_bitcast_fusion.18, f32[3,32,2,64,128]{4,1,3,2,0:T(8,128)S(1)} %convolution_bitcast_fusion.19, f32[3,32,2,64,128]{4,1,3,2,0:T(8,128)} %convolution_bitcast_fusion.20, f32[3,32,2,64,128]{4,1,3,2,0:T(8,128)} %convolution_bitcast_fusion.21, ...), kind=kLoop, calls=%fused_computation.129 | loop fusion | flops 6291456 | bytes 24084480 | tf_op jit(solution)/shard_map/convert_element_type | solution.py:146
  295.4 6.4 %collective-permute-done.8 = bf16[32,1,64,128]{3,0,2,1:T(8,128)(2,1)S(1)} collective-permute-done((bf16[32,1,64,128]{3,0,2,1:T(8,128)(2,1)S(1)}, bf16[32,1,64,128]{3,0,2,1:T(8,128)(2,1)S(1)}, u32[]{:S(2)}, u32[]{:S(2)}) %collective-permute-start.8) | collective-permute-done | bytes 524320 | tf_op jit(solution)/shard_map/ppermute | solution.py:25
  301.8 4.6 collective-permute-start.10
  334.5 13.9 %fusion.8 = (f32[32,2,64,128]{3,0,2,1:T(8,128)}, f32[32,2,64,128]{3,0,2,1:T(8,128)}) fusion(f32[3,32,2,64,128]{4,1,3,2,0:T(8,128)} %convolution_bitcast_fusion.9, f32[3,32,2,64,128]{4,1,3,2,0:T(8,128)S(1)} %convolution_bitcast_fusion.10, f32[3,32,2,64,128]{4,1,3,2,0:T(8,128)} %convolution_bitcast_fusion.11, ...), kind=kLoop, calls=%fused_computation.85 | loop fusion | flops 8388608 | bytes 41943040 | tf_op jit(solution)/shard_map/add | solution.py:112
  350.8 6.6 %fusion.13 = bf16[32,2,64,128]{3,0,2,1:T(8,128)(2,1)S(1)} fusion(f32[3,32,2,64,128]{4,1,3,2,0:T(8,128)} %convolution_bitcast_fusion.9, f32[3,32,2,64,128]{4,1,3,2,0:T(8,128)S(1)} %convolution_bitcast_fusion.10, f32[3,32,2,64,128]{4,1,3,2,0:T(8,128)} %convolution_bitcast_fusion.11, f32[3,32,2,64,128]{4,1,3,2,0:T(8,128)} %convolution_bitcast_fusion.12, ...), kind=kLoop, calls=%fused_computation.98 | loop fusion | flops 6291456 | bytes 24084480 | tf_op jit(solution)/shard_map/convert_element_type | solution.py:146
  366.1 5.2 %collective-permute-done.12 = bf16[32,1,64,128]{3,0,2,1:T(8,128)(2,1)S(1)} collective-permute-done((bf16[32,1,64,128]{3,0,2,1:T(8,128)(2,1)S(1)}, bf16[32,1,64,128]{3,0,2,1:T(8,128)(2,1)S(1)}, u32[]{:S(2)}, u32[]{:S(2)}) %collective-permute-start.12) | collective-permute-done | bytes 524320 | tf_op jit(solution)/shard_map/ppermute | solution.py:25
  371.2 4.3 collective-permute-start.14
  403.6 13.9 %fusion.1 = (f32[32,2,64,128]{3,0,2,1:T(8,128)}, f32[32,2,64,128]{3,0,2,1:T(8,128)}) fusion(f32[3,32,2,64,128]{4,1,3,2,0:T(8,128)} %convolution_bitcast_fusion, f32[3,32,2,64,128]{4,1,3,2,0:T(8,128)S(1)} %convolution_bitcast_fusion.1, f32[3,32,2,64,128]{4,1,3,2,0:T(8,128)} %convolution_bitcast_fusion.2, f32[3,32,2,64,128]{4,1,3,2,0:T(8,128)} %convolution_bitcast_fusion.3, ...), kind=kLoop, calls=%fused_computation.54 | loop fusion | flops 8388608 | bytes 41943040 | tf_op jit(solution)/shard_map/add | solution.py:112
  419.9 6.6 %fusion.6 = bf16[32,2,64,128]{3,0,2,1:T(8,128)(2,1)S(1)} fusion(f32[3,32,2,64,128]{4,1,3,2,0:T(8,128)} %convolution_bitcast_fusion, f32[3,32,2,64,128]{4,1,3,2,0:T(8,128)S(1)} %convolution_bitcast_fusion.1, f32[3,32,2,64,128]{4,1,3,2,0:T(8,128)} %convolution_bitcast_fusion.2, f32[3,32,2,64,128]{4,1,3,2,0:T(8,128)} %convolution_bitcast_fusion.3, ...), kind=kLoop, calls=%fused_computation.67 | loop fusion | flops 6291456 | bytes 24084480 | tf_op jit(solution)/shard_map/convert_element_type | solution.py:146
  435.2 4.7 %collective-permute-done.16 = bf16[32,1,64,128]{3,0,2,1:T(8,128)(2,1)S(1)} collective-permute-done((bf16[32,1,64,128]{3,0,2,1:T(8,128)(2,1)S(1)}, bf16[32,1,64,128]{3,0,2,1:T(8,128)(2,1)S(1)}, u32[]{:S(2)}, u32[]{:S(2)}) %collective-permute-start.16) | collective-permute-done | bytes 524320 | tf_op jit(solution)/shard_map/ppermute | solution.py:25
  439.9 4.5 collective-permute-start.18
  (170 shorter events, 211.4 us)
Async XLA Ops:
  7.2 53.9 %all-reduce.14.cloned.1.call-start = ((), (), s32[]{:S(2)}) async-start(), calls=%async_computation | async-start | bytes 1048576 | tf_op jit(solution)/shard_map/psum | solution.py:73
  17.3 97.8 %all-reduce.16.cloned.1.call-start = ((), (), s32[]{:S(2)}) async-start(), calls=%async_computation.1 | async-start | bytes 1048576 | tf_op jit(solution)/shard_map/psum | solution.py:73
  135.6 33.1 %copy-start.7 = (bf16[32,2,3,3,3]{0,1,4,3,2:T(2,128)(2,1)S(1)}, bf16[32,2,3,3,3]{0,1,4,3,2:T(2,128)(2,1)}, u32[]{:S(2)}) copy-start(bf16[32,2,3,3,3]{0,1,4,3,2:T(2,128)(2,1)} %param.11) | copy-start | bytes 10372
  164.4 5.4 %collective-permute-start.1 = (bf16[2,1,64,128]{3,2,1,0:T(8,128)(2,1)S(1)}, bf16[2,1,64,128]{3,2,1,0:T(8,128)(2,1)S(1)}, u32[]{:S(2)}, u32[]{:S(2)}) collective-permute-start(bf16[2,1,64,128]{3,2,1,0:T(8,128)(2,1)S(1)} %get-tuple-element.78), channel_id=1, source_target_pairs={{4,0},{8,4},{12,8},{16,12},{20,16},{24,20},{28,24},{5,1},{9,5},{13... | collective-permute-start | bytes 98312 | tf_op jit(solution)/shard_map/ppermute | solution.py:27
  166.3 6.0 %collective-permute-start = (bf16[2,1,64,128]{3,2,1,0:T(8,128)(2,1)S(1)}, bf16[2,1,64,128]{3,2,1,0:T(8,128)(2,1)S(1)}, u32[]{:S(2)}, u32[]{:S(2)}) collective-permute-start(bf16[2,1,64,128]{3,2,1,0:T(8,128)(2,1)S(1)} %get-tuple-element.77), channel_id=1, source_target_pairs={{0,4},{4,8},{8,12},{12,16},{16,20},{20,24},{24,28},{1,5},{5,9},{9,... | collective-permute-start | bytes 98312 | tf_op jit(solution)/shard_map/ppermute | solution.py:25
  172.3 5.2 %collective-permute-start.2 = (bf16[2,4,1,128]{3,2,1,0:T(2,128)(2,1)S(1)}, bf16[2,4,1,128]{3,2,1,0:T(2,128)(2,1)S(1)}, u32[]{:S(2)}, u32[]{:S(2)}) collective-permute-start(bf16[2,4,1,128]{3,2,1,0:T(2,128)(2,1)S(1)} %get-tuple-element.73), channel_id=1, source_target_pairs={{0,1},{1,2},{2,3},{4,5},{5,6},{6,7},{8,9},{9,10},{10,11},{12,13},{... | collective-permute-start | bytes 6152 | tf_op jit(solution)/shard_map/ppermute | solution.py:25
  173.9 5.5 %collective-permute-start.3 = (bf16[2,4,1,128]{3,2,1,0:T(2,128)(2,1)S(1)}, bf16[2,4,1,128]{3,2,1,0:T(2,128)(2,1)S(1)}, u32[]{:S(2)}, u32[]{:S(2)}) collective-permute-start(bf16[2,4,1,128]{3,2,1,0:T(2,128)(2,1)S(1)} %get-tuple-element.74), channel_id=1, source_target_pairs={{1,0},{2,1},{3,2},{5,4},{6,5},{7,6},{9,8},{10,9},{11,10},{13,12},{... | collective-permute-start | bytes 6152 | tf_op jit(solution)/shard_map/ppermute | solution.py:27
  215.3 4.6 copy-start.4
  215.4 8.7 %collective-permute-start.5 = (bf16[32,1,64,128]{3,0,2,1:T(8,128)(2,1)S(1)}, bf16[32,1,64,128]{3,0,2,1:T(8,128)(2,1)S(1)}, u32[]{:S(2)}, u32[]{:S(2)}) collective-permute-start(bf16[32,1,64,128]{3,0,2,1:T(8,128)(2,1)S(1)} %get-tuple-element.45), channel_id=1, source_target_pairs={{4,0},{8,4},{12,8},{16,12},{20,16},{24,20},{28,24},{5,1},{9,5},{13... | collective-permute-start | bytes 1572872 | tf_op jit(solution)/shard_map/ppermute | solution.py:27
  217.4 15.3 %collective-permute-start.4 = (bf16[32,1,64,128]{3,0,2,1:T(8,128)(2,1)S(1)}, bf16[32,1,64,128]{3,0,2,1:T(8,128)(2,1)S(1)}, u32[]{:S(2)}, u32[]{:S(2)}) collective-permute-start(bf16[32,1,64,128]{3,0,2,1:T(8,128)(2,1)S(1)} %get-tuple-element.44), channel_id=1, source_target_pairs={{0,4},{4,8},{8,12},{12,16},{16,20},{20,24},{24,28},{1,5},{5,9},{9,... | collective-permute-start | bytes 1572872 | tf_op jit(solution)/shard_map/ppermute | solution.py:25
  232.7 8.9 %collective-permute-start.6 = (bf16[32,4,1,128]{3,0,2,1:T(8,128)(2,1)S(1)}, bf16[32,4,1,128]{3,0,2,1:T(8,128)(2,1)S(1)}, u32[]{:S(2)}, u32[]{:S(2)}) collective-permute-start(bf16[32,4,1,128]{3,0,2,1:T(8,128)(2,1)S(1)} %get-tuple-element.32), channel_id=1, source_target_pairs={{0,1},{1,2},{2,3},{4,5},{5,6},{6,7},{8,9},{9,10},{10,11},{12,13},{... | collective-permute-start | bytes 98312 | tf_op jit(solution)/shard_map/ppermute | solution.py:25
  235.7 5.9 %collective-permute-start.7 = (bf16[32,4,1,128]{3,0,2,1:T(8,128)(2,1)S(1)}, bf16[32,4,1,128]{3,0,2,1:T(8,128)(2,1)S(1)}, u32[]{:S(2)}, u32[]{:S(2)}) collective-permute-start(bf16[32,4,1,128]{3,0,2,1:T(8,128)(2,1)S(1)} %get-tuple-element.33), channel_id=1, source_target_pairs={{1,0},{2,1},{3,2},{5,4},{6,5},{7,6},{9,8},{10,9},{11,10},{13,12},{... | collective-permute-start | bytes 98312 | tf_op jit(solution)/shard_map/ppermute | solution.py:27
  286.8 8.6 %collective-permute-start.9 = (bf16[32,1,64,128]{3,0,2,1:T(8,128)(2,1)S(1)}, bf16[32,1,64,128]{3,0,2,1:T(8,128)(2,1)S(1)}, u32[]{:S(2)}, u32[]{:S(2)}) collective-permute-start(bf16[32,1,64,128]{3,0,2,1:T(8,128)(2,1)S(1)} %get-tuple-element.43), channel_id=1, source_target_pairs={{4,0},{8,4},{12,8},{16,12},{20,16},{24,20},{28,24},{5,1},{9,5},{13... | collective-permute-start | bytes 1572872 | tf_op jit(solution)/shard_map/ppermute | solution.py:27
  288.7 13.1 %collective-permute-start.8 = (bf16[32,1,64,128]{3,0,2,1:T(8,128)(2,1)S(1)}, bf16[32,1,64,128]{3,0,2,1:T(8,128)(2,1)S(1)}, u32[]{:S(2)}, u32[]{:S(2)}) collective-permute-start(bf16[32,1,64,128]{3,0,2,1:T(8,128)(2,1)S(1)} %get-tuple-element.42), channel_id=1, source_target_pairs={{0,4},{4,8},{8,12},{12,16},{16,20},{20,24},{24,28},{1,5},{5,9},{9,... | collective-permute-start | bytes 1572872 | tf_op jit(solution)/shard_map/ppermute | solution.py:25
  301.8 10.5 %collective-permute-start.10 = (bf16[32,4,1,128]{3,0,2,1:T(8,128)(2,1)S(1)}, bf16[32,4,1,128]{3,0,2,1:T(8,128)(2,1)S(1)}, u32[]{:S(2)}, u32[]{:S(2)}) collective-permute-start(bf16[32,4,1,128]{3,0,2,1:T(8,128)(2,1)S(1)} %get-tuple-element.28), channel_id=1, source_target_pairs={{0,1},{1,2},{2,3},{4,5},{5,6},{6,7},{8,9},{9,10},{10,11},{12,13},{... | collective-permute-start | bytes 98312 | tf_op jit(solution)/shard_map/ppermute | solution.py:25
  306.4 5.9 %collective-permute-start.11 = (bf16[32,4,1,128]{3,0,2,1:T(8,128)(2,1)S(1)}, bf16[32,4,1,128]{3,0,2,1:T(8,128)(2,1)S(1)}, u32[]{:S(2)}, u32[]{:S(2)}) collective-permute-start(bf16[32,4,1,128]{3,0,2,1:T(8,128)(2,1)S(1)} %get-tuple-element.29), channel_id=1, source_target_pairs={{1,0},{2,1},{3,2},{5,4},{6,5},{7,6},{9,8},{10,9},{11,10},{13,12},{... | collective-permute-start | bytes 98312 | tf_op jit(solution)/shard_map/ppermute | solution.py:27
  357.4 8.6 %collective-permute-start.13 = (bf16[32,1,64,128]{3,0,2,1:T(8,128)(2,1)S(1)}, bf16[32,1,64,128]{3,0,2,1:T(8,128)(2,1)S(1)}, u32[]{:S(2)}, u32[]{:S(2)}) collective-permute-start(bf16[32,1,64,128]{3,0,2,1:T(8,128)(2,1)S(1)} %get-tuple-element.41), channel_id=1, source_target_pairs={{4,0},{8,4},{12,8},{16,12},{20,16},{24,20},{28,24},{5,1},{9,5},{13... | collective-permute-start | bytes 1572872 | tf_op jit(solution)/shard_map/ppermute | solution.py:27
  359.4 11.8 %collective-permute-start.12 = (bf16[32,1,64,128]{3,0,2,1:T(8,128)(2,1)S(1)}, bf16[32,1,64,128]{3,0,2,1:T(8,128)(2,1)S(1)}, u32[]{:S(2)}, u32[]{:S(2)}) collective-permute-start(bf16[32,1,64,128]{3,0,2,1:T(8,128)(2,1)S(1)} %get-tuple-element.40), channel_id=1, source_target_pairs={{0,4},{4,8},{8,12},{12,16},{16,20},{20,24},{24,28},{1,5},{5,9},{9,... | collective-permute-start | bytes 1572872 | tf_op jit(solution)/shard_map/ppermute | solution.py:25
  371.2 10.2 %collective-permute-start.14 = (bf16[32,4,1,128]{3,0,2,1:T(8,128)(2,1)S(1)}, bf16[32,4,1,128]{3,0,2,1:T(8,128)(2,1)S(1)}, u32[]{:S(2)}, u32[]{:S(2)}) collective-permute-start(bf16[32,4,1,128]{3,0,2,1:T(8,128)(2,1)S(1)} %get-tuple-element.24), channel_id=1, source_target_pairs={{0,1},{1,2},{2,3},{4,5},{5,6},{6,7},{8,9},{9,10},{10,11},{12,13},{... | collective-permute-start | bytes 98312 | tf_op jit(solution)/shard_map/ppermute | solution.py:25
  375.5 5.9 %collective-permute-start.15 = (bf16[32,4,1,128]{3,0,2,1:T(8,128)(2,1)S(1)}, bf16[32,4,1,128]{3,0,2,1:T(8,128)(2,1)S(1)}, u32[]{:S(2)}, u32[]{:S(2)}) collective-permute-start(bf16[32,4,1,128]{3,0,2,1:T(8,128)(2,1)S(1)} %get-tuple-element.25), channel_id=1, source_target_pairs={{1,0},{2,1},{3,2},{5,4},{6,5},{7,6},{9,8},{10,9},{11,10},{13,12},{... | collective-permute-start | bytes 98312 | tf_op jit(solution)/shard_map/ppermute | solution.py:27
  426.6 8.6 %collective-permute-start.17 = (bf16[32,1,64,128]{3,0,2,1:T(8,128)(2,1)S(1)}, bf16[32,1,64,128]{3,0,2,1:T(8,128)(2,1)S(1)}, u32[]{:S(2)}, u32[]{:S(2)}) collective-permute-start(bf16[32,1,64,128]{3,0,2,1:T(8,128)(2,1)S(1)} %get-tuple-element.39), channel_id=1, source_target_pairs={{4,0},{8,4},{12,8},{16,12},{20,16},{24,20},{28,24},{5,1},{9,5},{13... | collective-permute-start | bytes 1572872 | tf_op jit(solution)/shard_map/ppermute | solution.py:27
  428.5 11.4 %collective-permute-start.16 = (bf16[32,1,64,128]{3,0,2,1:T(8,128)(2,1)S(1)}, bf16[32,1,64,128]{3,0,2,1:T(8,128)(2,1)S(1)}, u32[]{:S(2)}, u32[]{:S(2)}) collective-permute-start(bf16[32,1,64,128]{3,0,2,1:T(8,128)(2,1)S(1)} %get-tuple-element.38), channel_id=1, source_target_pairs={{0,4},{4,8},{8,12},{12,16},{16,20},{20,24},{24,28},{1,5},{5,9},{9,... | collective-permute-start | bytes 1572872 | tf_op jit(solution)/shard_map/ppermute | solution.py:25
  439.9 6.8 %collective-permute-start.18 = (bf16[32,4,1,128]{3,0,2,1:T(8,128)(2,1)S(1)}, bf16[32,4,1,128]{3,0,2,1:T(8,128)(2,1)S(1)}, u32[]{:S(2)}, u32[]{:S(2)}) collective-permute-start(bf16[32,4,1,128]{3,0,2,1:T(8,128)(2,1)S(1)} %get-tuple-element.20), channel_id=1, source_target_pairs={{0,1},{1,2},{2,3},{4,5},{5,6},{6,7},{8,9},{9,10},{10,11},{12,13},{... | collective-permute-start | bytes 98312 | tf_op jit(solution)/shard_map/ppermute | solution.py:25
  444.5 5.8 %collective-permute-start.19 = (bf16[32,4,1,128]{3,0,2,1:T(8,128)(2,1)S(1)}, bf16[32,4,1,128]{3,0,2,1:T(8,128)(2,1)S(1)}, u32[]{:S(2)}, u32[]{:S(2)}) collective-permute-start(bf16[32,4,1,128]{3,0,2,1:T(8,128)(2,1)S(1)} %get-tuple-element.21), channel_id=1, source_target_pairs={{1,0},{2,1},{3,2},{5,4},{6,5},{7,6},{9,8},{10,9},{11,10},{13,12},{... | collective-permute-start | bytes 98312 | tf_op jit(solution)/shard_map/ppermute | solution.py:27
  (7 other events, 15.8 us)
Sparse Core Ops, SparseCore 0:
  17.4 43.5 all-reduce.13
  76.5 38.5 all-reduce.15
